TPU v7x, 256 devices: a whole 4x4x8 slice. The times are simulated.
256 devices in a mesh: region: 8 (over x, core), dom: 32 (over z, y).
Axes of the slice: x: 4, y: 4, z: 8, core: 2. Of those that a mesh axis runs over, the one named last changes fastest.
Arguments:
- x_init: bfloat16 [1048576, 128], P(('region', 'dom')), may hold values from -6 to 6
- tiles: bfloat16 [73728, 128, 128], P(('region', 'dom'))
- tile_row: int32 [73728], P(('region', 'dom')), may hold values from 0 to 31
- tile_col: int32 [73728], P(('region', 'dom')), may hold values from 0 to 63, as said below
- send_list: int32 [256, 4, 8], P(('region', 'dom')), may hold values from 0 to 31, as said below
- send_count: int32 [256, 4], P(('region', 'dom')), may hold values from 1 to 8, as said below
Outputs:
- basis: bfloat16 [1048576, 128], P(('region', 'dom'))
- ritz_matrix: float32 [2, 128, 128], replicated
Inputs may be any that keep to these rules, and one draw needn't show every extreme that they name: `send_list`: the 8 entries of one partition and direction are distinct row tiles of that partition. `send_count`: some partition sends 8 row tiles in every direction. `tile_col`: a value 32 + d * 8 + s with d = 0 .. 3 names slot s of the d-th received stack of extended, and s is below the count that this neighbour sends; no value names a stack where the neighbour does not exist.
All inputs are finite; a program needn't handle non-finite values.
Results may differ from a plain program's by a relative error of at most 0.00115.
The roundings to bfloat16 on the way count: a program that leaves them out, or rounds other values in their place, can miss the bound.
Values may be sent and summed in bfloat16 or wider, within the bound.
No kernel may reach another device: no remote copies, remote signals or barrier semaphores. Data moves between devices by JAX's collectives and lax.ppermute only.
A program may use at most 64 MiB of HBM per device.

v0:
```python
import math
import jax
import jax.numpy as jnp
from jax import lax
from jax.sharding import PartitionSpec as P

ITERS = 2
HIGH = lax.Precision.HIGHEST


def shifted(block, axis, distance):
    devices = range(lax.axis_size(axis))
    route = [(i - distance, i) for i in devices if i - distance in devices]
    return lax.ppermute(block, axis, route)


def local_gram(current, node_total):
    return (
        lax.dot_general(
            current, current, (((0,), (0,)), ((), ())), preferred_element_type=jnp.float32
        )
        / node_total
    )


def rayleigh_sum(partial_value):
    return lax.psum(partial_value, ("region", "dom"))


def pass_dom(packed, offset):
    return shifted(packed, "dom", offset)


def pass_region(packed, offset):
    return shifted(packed, "region", offset)


def apply_graph(basis, tiles, tile_row, tile_col, send_rows, live_slot, row_tiles, tile_size):
    vectors = basis.shape[1]
    blocks = basis.reshape(row_tiles, tile_size, vectors)
    picked = blocks[send_rows]
    packed = jnp.where(live_slot[:, :, None, None], picked, jnp.zeros_like(picked))
    received = [
        pass_dom(packed[0], 1),
        pass_dom(packed[1], -1),
        pass_region(packed[2], 1),
        pass_region(packed[3], -1),
    ]
    extended = jnp.concatenate([blocks] + received, axis=0)
    group = 32
    group_count = tiles.shape[0] // group
    tile_groups = tiles.reshape(group_count, group, tile_size, tile_size)
    col_groups = tile_col.reshape(group_count, group)
    row_groups = tile_row.reshape(group_count, group)
    row_ids = jnp.arange(row_tiles, dtype=jnp.int32)

    def add_group(accumulated, pieces):
        tile_part, col_part, row_part = pieces
        gathered = extended[col_part]
        products = lax.dot_general(
            tile_part, gathered, (((2,), (1,)), ((0,), (0,))), preferred_element_type=jnp.float32
        )
        select = (row_part[None, :] == row_ids[:, None]).astype(jnp.float32)
        return (accumulated + jnp.einsum("rt,tiw->riw", select, products, precision=HIGH), None)

    start = jnp.zeros((row_tiles, tile_size, vectors), jnp.float32)
    applied, _ = lax.scan(add_group, start, (tile_groups, col_groups, row_groups))
    return applied.reshape(row_tiles * tile_size, vectors)


def shards(x_init, tiles, tile_row, tile_col, send_list, send_count):
    row_count, vectors = x_init.shape
    tile_size = tiles.shape[1]
    row_tiles = row_count // tile_size
    capacity = send_list.shape[2]
    node_total = row_count * lax.axis_size("region") * lax.axis_size("dom")
    root_total = math.sqrt(node_total)
    send_rows = send_list[0]
    live_slot = jnp.arange(capacity, dtype=jnp.int32)[None, :] < send_count[0][:, None]
    identity = jnp.eye(vectors, dtype=jnp.float32)
    current = x_init
    gram = lax.psum(local_gram(current, node_total), ("region", "dom"))
    rayleigh_list = []
    basis = x_init
    for iteration in range(ITERS):
        factor = jnp.linalg.cholesky(gram)
        inverse = lax.linalg.triangular_solve(factor, identity, left_side=True, lower=True)
        basis = jnp.dot(current.astype(jnp.float32), inverse.T, precision=HIGH).astype(jnp.bfloat16)
        applied = apply_graph(
            basis, tiles, tile_row, tile_col, send_rows, live_slot, row_tiles, tile_size
        )
        partial_value = jnp.dot(basis.astype(jnp.float32).T, applied, precision=HIGH) / root_total
        if iteration + 1 < ITERS:
            current = applied.astype(jnp.bfloat16)
            rayleigh_list.append(rayleigh_sum(partial_value))
            gram = lax.psum(local_gram(current, node_total), ("region", "dom"))
        else:
            rayleigh_list.append(rayleigh_sum(partial_value))
    return (basis, jnp.stack(rayleigh_list))


def solution(mesh):
    in_specs = (
        P(("region", "dom"), None),
        P(("region", "dom"), None, None),
        P(("region", "dom")),
        P(("region", "dom")),
        P(("region", "dom"), None, None),
        P(("region", "dom"), None),
    )
    out_specs = (P(("region", "dom"), None), P())
    return jax.shard_map(shards, mesh=mesh, in_specs=in_specs, out_specs=out_specs, check_vma=False)
```

profile of v0, /device:TPU:2, one launch (start us, length us, event | category | flops | bytes accessed | tf_op | source)
XLA Modules:
  0.0 1021.1 jit_solution(12112515196211047036)
XLA Ops:
  9.8 247.8 %all-reduce.5.cloned.1.call-done = f32[128,128]{0,1:T(8,128)} async-done(((f32[128,128]{0,1:T(8,128)}), f32[128,128]{0,1:T(8,128)}) %all-reduce.5.cloned.1.call-update) | async-done | bytes 65552 | tf_op jit(solution)/shard_map/psum | solution.py:82
  259.4 11.7 %cholesky.44 = f32[128,128]{1,0:T(8,128)S(1)} custom-call(f32[128,128]{1,0:T(8,128)S(1)} %fusion.46), custom_call_target="Cholesky" | custom-call | tf_op jit(solution)/shard_map/jit(cholesky)/cholesky | solution.py:86
  272.4 9.8 custom-call.8
  303.6 82.5 %while.22 = (s32[]{:T(128)}, f32[32,128,128]{2,0,1:T(8,128)}, s32[9,32]{1,0:T(8,128)S(1)}, bf16[9,32,128,128]{3,2,1,0:T(8,128)(2,1)}, s32[9,32]{1,0:T(8,128)S(1)...) while((s32[]{:T(128)}, f32[32,128,128]{2,0,1:T(8,128)}, s32[9,32]{1,0:T(8,128)S(1)}, ...), condition=%wide.region_4.7_spmd.clone, body=%wide.region_3.6_spmd.clone.sunk | while | flops 336595040 | bytes 29365292 | solution.py:67
  307.8 3.5 select_add_fusion.4
  317.0 3.5 select_add_fusion.4
  326.2 3.5 select_add_fusion.4
  335.4 3.5 select_add_fusion.4
  353.7 3.5 select_add_fusion.4
  362.9 3.5 select_add_fusion.4
  372.0 3.5 select_add_fusion.4
  392.2 239.2 %all-reduce.7.cloned.1.call-done = f32[128,128]{0,1:T(8,128)} async-done(((f32[128,128]{0,1:T(8,128)}), f32[128,128]{0,1:T(8,128)}) %all-reduce.7.cloned.1.call-update) | async-done | bytes 65552 | tf_op jit(solution)/shard_map/psum | solution.py:96
  633.2 11.7 %cholesky.55 = f32[128,128]{1,0:T(8,128)S(1)} custom-call(f32[128,128]{1,0:T(8,128)S(1)} %fusion.44), custom_call_target="Cholesky" | custom-call | tf_op jit(solution)/shard_map/jit(cholesky)/cholesky | solution.py:86
  646.3 9.8 custom-call.9
  661.5 4.6 collective-permute-start.4
  670.0 3.9 collective-permute-start.7
  678.8 82.3 %while.23 = (s32[]{:T(128)}, f32[32,128,128]{2,0,1:T(8,128)}, s32[9,32]{1,0:T(8,128)S(1)}, bf16[9,32,128,128]{3,2,1,0:T(8,128)(2,1)}, s32[9,32]{1,0:T(8,128)S(1)...) while((s32[]{:T(128)}, f32[32,128,128]{2,0,1:T(8,128)}, s32[9,32]{1,0:T(8,128)S(1)}, ...), condition=%wide.region_8.11_spmd.clone, body=%wide.region_7.10_spmd.clone.sunk | while | flops 336595040 | bytes 29365292 | solution.py:67
  683.1 3.5 select_add_fusion.5
  692.2 3.5 select_add_fusion.5
  701.4 3.5 select_add_fusion.5
  710.5 3.5 select_add_fusion.5
  719.7 3.5 select_add_fusion.5
  756.3 3.5 select_add_fusion.5
  766.0 247.0 %all-reduce.9.cloned.1.call-done = (f32[1,128,128]{2,1,0:T(8,128)}, f32[1,128,128]{2,1,0:T(8,128)}) async-done(((f32[1,128,128]{2,1,0:T(8,128)}, f32[1,128,128]{2,1,0:T(8,128)}), (f32[1,128,128]{2,1,0:T(8,128)}, f32[1,128,128]{2,1,0:T(8,128)})) %all-reduce.9.cloned.1.call-update) | async-done | bytes 131088 | tf_op jit(solution)/shard_map/psum | solution.py:27
  (257 shorter events, 174.8 us)
Async XLA Ops:
  7.2 2.4 copy-start.15
  7.2 2.5 copy-start.14
  7.2 250.4 %all-reduce.5.cloned.1.call-start = ((), (), s32[]{:S(2)}) async-start(), calls=%async_computation | async-start | bytes 131072 | tf_op jit(solution)/shard_map/psum | solution.py:82
  9.5 621.9 %all-reduce.7.cloned.1.call-start = ((), (), s32[]{:S(2)}) async-start(), calls=%async_computation.1 | async-start | bytes 131072 | tf_op jit(solution)/shard_map/psum | solution.py:96
  283.5 2.3 copy-start.10
  285.9 6.6 copy-start.12
  285.9 6.7 copy-start.13
  288.2 10.3 %collective-permute-start = (bf16[8,128,128]{2,1,0:T(8,128)(2,1)}, bf16[8,128,128]{2,1,0:T(8,128)(2,1)S(1)}, u32[]{:S(2)}, u32[]{:S(2)}) collective-permute-start(bf16[8,128,128]{2,1,0:T(8,128)(2,1)} %get-tuple-element.159), channel_id=1, source_target_pairs={{0,1},{1,2},{2,3},{3,4},{4,5},{5,6},{6,7},{7,8},{8,9},{9,10},{10,1... | collective-permute-start | bytes 786440 | tf_op jit(solution)/shard_map/ppermute | solution.py:14
  291.2 10.8 %collective-permute-start.1 = (bf16[8,128,128]{2,1,0:T(8,128)(2,1)}, bf16[8,128,128]{2,1,0:T(8,128)(2,1)S(1)}, u32[]{:S(2)}, u32[]{:S(2)}) collective-permute-start(bf16[8,128,128]{2,1,0:T(8,128)(2,1)} %get-tuple-element.158), channel_id=1, source_target_pairs={{1,0},{2,1},{3,2},{4,3},{5,4},{6,5},{7,6},{8,7},{9,8},{10,9},{11,1... | collective-permute-start | bytes 786440 | tf_op jit(solution)/shard_map/ppermute | solution.py:14
  292.6 9.4 collective-permute-start.2
  295.1 7.0 collective-permute-start.3
  324.3 1.9 copy-start.1
  333.4 1.9 copy-start.1
  386.1 3.6 copy-start.3
  389.6 623.4 %all-reduce.9.cloned.1.call-start = ((), (), s32[]{:S(2)}) async-start(), calls=%async_computation.2 | async-start | bytes 262144 | tf_op jit(solution)/shard_map/psum | solution.py:27
  659.0 105.0 %copy-start.9 = (bf16[4096,128]{1,0:T(8,128)(2,1)}, bf16[4096,128]{1,0:T(8,128)(2,1)S(1)}, u32[]{:S(2)}) copy-start(bf16[4096,128]{1,0:T(8,128)(2,1)S(1)} %convolution_convert_fusion) | copy-start | bytes 3145732
  659.7 6.3 copy-start.8
  659.8 6.3 copy-start.11
  660.0 13.9 %collective-permute-start.5 = (bf16[8,128,128]{2,1,0:T(8,128)(2,1)S(1)}, bf16[8,128,128]{2,1,0:T(8,128)(2,1)S(1)}, u32[]{:S(2)}, u32[]{:S(2)}) collective-permute-start(bf16[8,128,128]{2,1,0:T(8,128)(2,1)S(1)} %get-tuple-element.154), channel_id=1, source_target_pairs={{1,0},{2,1},{3,2},{4,3},{5,4},{6,5},{7,6},{8,7},{9,8},{10,9},{11,1... | collective-permute-start | bytes 786440 | tf_op jit(solution)/shard_map/ppermute | solution.py:14
  661.5 12.4 %collective-permute-start.4 = (bf16[8,128,128]{2,1,0:T(8,128)(2,1)S(1)}, bf16[8,128,128]{2,1,0:T(8,128)(2,1)S(1)}, u32[]{:S(2)}, u32[]{:S(2)}) collective-permute-start(bf16[8,128,128]{2,1,0:T(8,128)(2,1)S(1)} %get-tuple-element.155), channel_id=1, source_target_pairs={{0,1},{1,2},{2,3},{3,4},{4,5},{5,6},{6,7},{7,8},{8,9},{9,10},{10,1... | collective-permute-start | bytes 786440 | tf_op jit(solution)/shard_map/ppermute | solution.py:14
  667.9 7.7 collective-permute-start.6
  670.0 7.5 collective-permute-start.7
  681.2 1.9 copy-start.4
  690.3 1.9 copy-start.4
  (35 other events, 54.9 us)
Sparse Core Ops, SparseCore 0:
  14.1 243.4 all-reduce.4
  389.7 241.6 all-reduce.6
  766.1 246.8 all-reduce.8
where the time goes:
time: 1020 us
  waiting for transfers between devices  741 us (73%)
  matrix products  108 us (11%)
  local copies, waits for them, and re-layouts  83.8 us (8%)
  other arithmetic  50.8 us (5%)
  starting transfers between devices  21.9 us (2%)
  between operations  14.2 us (1%)
    psum x2, waiting for transfers between devices, shards(): gram = lax.psum(local_gram(current, node_total), ('region', 'dom'))  487 us
    psum x1, waiting for transfers between devices, rayleigh_sum(): return lax.psum(partial_value, ('region', 'dom'))  247 us
    dot_general x18, matrix products, add_group(): jnp.einsum('rt,tiw->riw', select, products, precision=HIGH)  63.3 us
    gather x18, local copies, waits for them, and re-layouts, add_group(): gathered = extended[col_part]  42.1 us
    dot_general x18, matrix products, add_group(): lax.dot_general(tile_part, gathered, (((2,), (1,)), ((0,), (0,))), prefer...  32.4 us
    while x72, local copies, waits for them, and re-layouts  25.8 us
    another operation x6, other arithmetic, shards(): factor = jnp.linalg.cholesky(gram)  24.8 us
    ppermute x8, starting transfers between devices, shifted(): return lax.ppermute(block, axis, route)  21.8 us
  transfers between devices with their start and end apart: 11, of which 7 were waited for; matrix products, arithmetic and copies ran while one was open for 1% of the time, Pallas kernels for 0%

commit v1 on v0

--- a/solution.py
+++ b/solution.py
@@ -93,7 +93,7 @@
         if iteration + 1 < ITERS:
             current = applied.astype(jnp.bfloat16)
             rayleigh_list.append(rayleigh_sum(partial_value))
-            gram = lax.psum(local_gram(current, node_total), ("region", "dom"))
+            gram = jnp.sum(lax.all_gather(local_gram(current, node_total), ("region", "dom")), 0)
         else:
             rayleigh_list.append(rayleigh_sum(partial_value))
     return (basis, jnp.stack(rayleigh_list))

time: 1020 us -> 940 us (0.922)
  waiting for transfers between devices: 741 us -> 633 us
  matrix products: 108 us -> 135 us
    psum x2 -> x1, waiting for transfers between devices: 487 us -> 248 us  [shards(): gram = lax.psum(local_gram(current, node_total), ('region', 'dom'))]
    all_gather x0 -> x1, waiting for transfers between devices: none -> 135 us  [shards(): lax.all_gather(local_gram(current, node_total), ('region', 'dom'))]
    dot_general x18, matrix products: 63.3 us -> 94.5 us  [add_group(): jnp.einsum('rt,tiw->riw', select, products, precision=HIGH)]
    while x72 -> x0, local copies, waits for them, and re-layouts: 25.8 us -> none
    unnamed x32 -> x33, local copies, waits for them, and re-layouts: 4.23 us -> 21.9 us
  transfers between devices with their start and end apart: 11 -> 11, of which waited for: 7 -> 5; matrix products, arithmetic and copies ran while one was open for 1% -> 1% of each run, Pallas kernels for 0% -> 0%
where the time goes in v1:
time: 940 us; the launch traced here: 937 us
  waiting for transfers between devices  633 us (67%)
  matrix products  135 us (14%)
  local copies, waits for them, and re-layouts  75.7 us (8%)
  other arithmetic  58.3 us (6%)
  starting transfers between devices  20.6 us (2%)
  between operations  14.1 us (2%)
    psum x1, waiting for transfers between devices, shards(): gram = lax.psum(local_gram(current, node_total), ('region', 'dom'))  248 us
    psum x1, waiting for transfers between devices, rayleigh_sum(): return lax.psum(partial_value, ('region', 'dom'))  247 us
    all_gather x1, waiting for transfers between devices, shards(): lax.all_gather(local_gram(current, node_total), ('region', 'dom'))  135 us
    dot_general x18, matrix products, add_group(): jnp.einsum('rt,tiw->riw', select, products, precision=HIGH)  94.5 us
    gather x18, local copies, waits for them, and re-layouts, add_group(): gathered = extended[col_part]  42.1 us
    dot_general x18, matrix products, add_group(): lax.dot_general(tile_part, gathered, (((2,), (1,)), ((0,), (0,))), prefer...  29.8 us
    another operation x6, other arithmetic, shards(): factor = jnp.linalg.cholesky(gram)  24.8 us
    unnamed x33, local copies, waits for them, and re-layouts  21.9 us
  transfers between devices with their start and end apart: 11, of which 5 were waited for; matrix products, arithmetic and copies ran while one was open for 1% of the time, Pallas kernels for 0%

profile of v1, /device:TPU:2, one launch (start us, length us, event | category | flops | bytes accessed | tf_op | source)
XLA Modules:
  0.0 937.5 jit_solution(10605159129228070745)
XLA Ops:
  9.8 247.8 %all-reduce.4.cloned.1.call-done = f32[128,128]{0,1:T(8,128)} async-done(((f32[128,128]{0,1:T(8,128)}), f32[128,128]{0,1:T(8,128)}) %all-reduce.4.cloned.1.call-update) | async-done | bytes 65552 | tf_op jit(solution)/shard_map/psum | solution.py:82
  259.4 11.7 %cholesky.44 = f32[128,128]{1,0:T(8,128)S(1)} custom-call(f32[128,128]{1,0:T(8,128)S(1)} %fusion.46), custom_call_target="Cholesky" | custom-call | tf_op jit(solution)/shard_map/jit(cholesky)/cholesky | solution.py:86
  272.4 9.8 %custom-call.8 = f32[1,128,128]{1,2,0:T(8,128)S(1)} custom-call(f32[1,128,128]{2,1,0:T(8,128)S(1)} %fusion.41), custom_call_target="InvertDiagBlocksLowerTriangular" | custom-call | tf_op jit(solution)/shard_map/triangular_solve/custom-call.0 | solution.py:87
  301.1 83.7 %while.22 = (s32[]{:T(128)}, f32[32,128,128]{2,0,1:T(8,128)}, s32[9,32]{1,0:T(8,128)S(1)}, bf16[9,32,128,128]{3,2,1,0:T(8,128)(2,1)}, s32[9,32]{1,0:T(8,128)S(1)...) while((s32[]{:T(128)}, f32[32,128,128]{2,0,1:T(8,128)}, s32[9,32]{1,0:T(8,128)S(1)}, ...), condition=%wide.region_4.7_spmd.clone, body=%wide.region_3.6_spmd.clone.sunk | while | flops 336595040 | bytes 12588519 | solution.py:67
  313.0 5.4 select_add_fusion.4
  322.5 5.4 select_add_fusion.4
  332.0 5.4 select_add_fusion.4
  341.4 5.4 select_add_fusion.4
  350.9 5.4 select_add_fusion.4
  360.4 5.4 select_add_fusion.4
  369.9 5.4 select_add_fusion.4
  379.4 5.4 select_add_fusion.4
  391.0 134.6 %all-gather.3.cloned.1.call-done = f32[32768,128]{0,1:T(8,128)} async-done(((f32[128,128]{0,1:T(8,128)}), f32[32768,128]{0,1:T(8,128)}) %all-gather.3.cloned.1.call-update) | async-done | bytes 16777232 | tf_op jit(solution)/shard_map/all_gather | solution.py:96
  525.6 14.1 %copy.34 = f32[16,8,256,128]{3,2,1,0:T(8,128)} copy(f32[16,8,256,128]{3,1,2,0:T(8,128)} %bitcast.131) | data formatting | bytes 33554432
  539.7 8.2 bitcast_reduce_fusion
  548.0 11.7 %cholesky.55 = f32[128,128]{1,0:T(8,128)S(1)} custom-call(f32[128,128]{1,0:T(8,128)S(1)} %fusion.44), custom_call_target="Cholesky" | custom-call | tf_op jit(solution)/shard_map/jit(cholesky)/cholesky | solution.py:86
  561.1 9.8 %custom-call.9 = f32[1,128,128]{1,2,0:T(8,128)S(1)} custom-call(f32[1,128,128]{2,1,0:T(8,128)S(1)} %fusion.42), custom_call_target="InvertDiagBlocksLowerTriangular" | custom-call | tf_op jit(solution)/shard_map/triangular_solve/custom-call.0 | solution.py:87
  593.5 83.6 %while.23 = (s32[]{:T(128)}, f32[32,128,128]{2,0,1:T(8,128)}, s32[9,32]{1,0:T(8,128)S(1)}, bf16[9,32,128,128]{3,2,1,0:T(8,128)(2,1)}, s32[9,32]{1,0:T(8,128)S(1)...) while((s32[]{:T(128)}, f32[32,128,128]{2,0,1:T(8,128)}, s32[9,32]{1,0:T(8,128)S(1)}, ...), condition=%wide.region_8.11_spmd.clone, body=%wide.region_7.10_spmd.clone.sunk | while | flops 336595040 | bytes 12588519 | solution.py:67
  605.5 5.4 select_add_fusion.5
  614.9 5.4 select_add_fusion.5
  624.4 5.4 select_add_fusion.5
  633.9 5.4 select_add_fusion.5
  671.7 5.4 select_add_fusion.5
  682.1 247.3 %all-reduce.6.cloned.1.call-done = (f32[1,128,128]{2,1,0:T(8,128)}, f32[1,128,128]{2,1,0:T(8,128)}) async-done(((f32[1,128,128]{2,1,0:T(8,128)}, f32[1,128,128]{2,1,0:T(8,128)}), (f32[1,128,128]{2,1,0:T(8,128)}, f32[1,128,128]{2,1,0:T(8,128)})) %all-reduce.6.cloned.1.call-update) | async-done | bytes 131088 | tf_op jit(solution)/shard_map/psum | solution.py:27
  (187 shorter events, 157.3 us)
Async XLA Ops:
  7.2 1.2 copy-start
  7.2 2.4 copy-start.10
  7.2 2.5 copy-start.11
  7.2 250.4 %all-reduce.4.cloned.1.call-start = ((), (), s32[]{:S(2)}) async-start(), calls=%async_computation | async-start | bytes 131072 | tf_op jit(solution)/shard_map/psum | solution.py:82
  9.5 516.1 %all-gather.3.cloned.1.call-start = ((), (), s32[]{:S(2)}) async-start(), calls=%async_computation.1 | async-start | bytes 16842752 | tf_op jit(solution)/shard_map/all_gather | solution.py:96
  283.5 1.4 copy-start.6
  285.0 4.6 copy-start.8
  285.0 4.6 copy-start.9
  285.2 11.3 %collective-permute-start = (bf16[8,128,128]{2,1,0:T(8,128)(2,1)S(1)}, bf16[8,128,128]{2,1,0:T(8,128)(2,1)S(1)}, u32[]{:S(2)}, u32[]{:S(2)}) collective-permute-start(bf16[8,128,128]{2,1,0:T(8,128)(2,1)S(1)} %get-tuple-element.159), channel_id=1, source_target_pairs={{0,1},{1,2},{2,3},{3,4},{4,5},{5,6},{6,7},{7,8},{8,9},{9,10},{10,1... | collective-permute-start | bytes 786440 | tf_op jit(solution)/shard_map/ppermute | solution.py:14
  288.2 10.6 %collective-permute-start.1 = (bf16[8,128,128]{2,1,0:T(8,128)(2,1)S(1)}, bf16[8,128,128]{2,1,0:T(8,128)(2,1)S(1)}, u32[]{:S(2)}, u32[]{:S(2)}) collective-permute-start(bf16[8,128,128]{2,1,0:T(8,128)(2,1)S(1)} %get-tuple-element.158), channel_id=1, source_target_pairs={{1,0},{2,1},{3,2},{4,3},{5,4},{6,5},{7,6},{8,7},{9,8},{10,9},{11,1... | collective-permute-start | bytes 786440 | tf_op jit(solution)/shard_map/ppermute | solution.py:14
  289.7 9.9 %collective-permute-start.2 = (bf16[8,128,128]{2,1,0:T(8,128)(2,1)S(1)}, bf16[8,128,128]{2,1,0:T(8,128)(2,1)S(1)}, u32[]{:S(2)}, u32[]{:S(2)}) collective-permute-start(bf16[8,128,128]{2,1,0:T(8,128)(2,1)S(1)} %get-tuple-element.157), channel_id=1, source_target_pairs={{0,32},{32,64},{64,96},{96,128},{128,160},{160,192},{192,224},{1,3... | collective-permute-start | bytes 786440 | tf_op jit(solution)/shard_map/ppermute | solution.py:14
  293.2 7.1 collective-permute-start.3
  384.8 3.6 copy-start.2
  388.3 541.1 %all-reduce.6.cloned.1.call-start = ((), (), s32[]{:S(2)}) async-start(), calls=%async_computation.2 | async-start | bytes 262144 | tf_op jit(solution)/shard_map/psum | solution.py:27
  539.7 31.5 %copy-start.3 = (f32[32,128,128]{2,1,0:T(8,128)S(1)}, f32[32,128,128]{2,1,0:T(8,128)}, u32[]{:S(2)}) copy-start(f32[32,128,128]{2,1,0:T(8,128)} %copy.20) | copy-start | bytes 6291460
  572.2 12.0 %copy-start.4 = (bf16[4096,128]{1,0:T(8,128)(2,1)}, bf16[4096,128]{1,0:T(8,128)(2,1)S(1)}, u32[]{:S(2)}) copy-start(bf16[4096,128]{1,0:T(8,128)(2,1)S(1)} %convolution_convert_fusion) | copy-start | bytes 3145732
  573.9 6.5 copy-start.7
  575.4 13.5 %collective-permute-start.4 = (bf16[8,128,128]{2,1,0:T(8,128)(2,1)S(1)}, bf16[8,128,128]{2,1,0:T(8,128)(2,1)S(1)}, u32[]{:S(2)}, u32[]{:S(2)}) collective-permute-start(bf16[8,128,128]{2,1,0:T(8,128)(2,1)S(1)} %get-tuple-element.155), channel_id=1, source_target_pairs={{0,1},{1,2},{2,3},{3,4},{4,5},{5,6},{6,7},{7,8},{8,9},{9,10},{10,1... | collective-permute-start | bytes 786440 | tf_op jit(solution)/shard_map/ppermute | solution.py:14
  578.8 10.8 %collective-permute-start.5 = (bf16[8,128,128]{2,1,0:T(8,128)(2,1)S(1)}, bf16[8,128,128]{2,1,0:T(8,128)(2,1)S(1)}, u32[]{:S(2)}, u32[]{:S(2)}) collective-permute-start(bf16[8,128,128]{2,1,0:T(8,128)(2,1)S(1)} %get-tuple-element.154), channel_id=1, source_target_pairs={{1,0},{2,1},{3,2},{4,3},{5,4},{6,5},{7,6},{8,7},{9,8},{10,9},{11,1... | collective-permute-start | bytes 786440 | tf_op jit(solution)/shard_map/ppermute | solution.py:14
  582.3 8.2 collective-permute-start.6
  585.3 7.5 collective-permute-start.7
  677.1 3.0 copy-start.5
  677.1 253.8 %copy-start.1 = (bf16[4096,128]{1,0:T(8,128)(2,1)S(1)}, bf16[4096,128]{1,0:T(8,128)(2,1)}, u32[]{:S(2)}) copy-start(bf16[4096,128]{1,0:T(8,128)(2,1)} %param.13) | copy-start | bytes 3145732
Sparse Core Ops, SparseCore 0:
  14.1 243.4 all-reduce.3
  388.4 137.1 all-gather.2
  682.3 247.0 all-reduce.5
